TPU v7x, 32 devices: a whole 2x2x4 slice. The times are simulated.
32 devices in a mesh: groups: 2 (over x), blk: 16 (over z, y, core).
Axes of the slice: x: 2, y: 2, z: 4, core: 2. Of those that a mesh axis runs over, the one named last changes fastest.
Arguments:
- hidden: bfloat16 [16384, 2048], P(('groups', 'blk')), parts along dimension 0, may hold values from -6 to 6
- kept_idx: int32 [32, 128], P(('groups', 'blk')), parts along dimension 0, may hold values from 0 to 511, as said below
- kept_count: int32 [32], P(('groups', 'blk')), parts along dimension 0, may hold values from 0 to 128, as said below
- router: bfloat16 [2048], replicated, may hold values from -0.125 to 0.125
- norm_gain: float32 [2048], replicated, may hold values from 0.25 to 1.75
- qk_gain: float32 [2, 64], replicated, may hold values from 1 to 7
- query_weight: bfloat16 [2048, 2048], P('blk'), may hold values from -1 to 1
- key_weight: bfloat16 [2048, 128], P('blk'), may hold values from -1 to 1
- value_weight: bfloat16 [2048, 128], P('blk'), may hold values from -0.125 to 0.125
- out_weight: bfloat16 [2048, 2048], P('blk'), may hold values from -0.375 to 0.375
Outputs:
- mixed: bfloat16 [16384, 2048], P(('groups', 'blk')), parts along dimension 0
There are 2 independent parts, one for each index of `groups`. A program takes and returns all parts, laid end to end along the dimension named above; an argument that names none is the same for every part. Nothing has to cross between parts.
Inputs may be any that keep to these rules, and one draw needn't show every extreme that they name: `kept_count`: the counts sum to 1024; in every draw some shard's count is exactly 128. `kept_idx`: in row s the first kept_count[s] entries are distinct local token indices in increasing order; entries past the count are 0.
All inputs are finite; a program needn't handle non-finite values.
Results may differ from a plain program's by a relative error of at most 0.01.
Values may be sent and summed in bfloat16 or wider, within the bound.
A program may use at most 128 MiB of HBM per device.

v0:
```python
import math
import jax
import jax.numpy as jnp
from jax import lax
from jax.sharding import PartitionSpec as P

Q_HEADS = 32
KV_HEADS = 2
HEAD = 64
TOK_DEV = 512
KEEP_DEV = 64
CAP = 128
norm_eps = 1e-06
rope_base = 1000000.0


def rms_scale(values, scales):
    return values * lax.rsqrt(jnp.mean(values * values, axis=-1, keepdims=True) + norm_eps) * scales


def rotate(values, angles):
    half_size = values.shape[-1] // 2
    lower_half = values[..., :half_size]
    upper_half = values[..., half_size:]
    cosine = jnp.cos(angles)
    sine_part = jnp.sin(angles)
    return jnp.concatenate(
        [
            lower_half * cosine - upper_half * sine_part,
            upper_half * cosine + lower_half * sine_part,
        ],
        axis=-1,
    )


def attend(query_heads, query_ranks, key_block, value_block, key_ranks, state):
    prev_top, prev_total, prev_acc = state
    length = key_block.shape[0]
    keys_split = key_block.reshape(length, KV_HEADS, HEAD)
    values_split = value_block.reshape(length, KV_HEADS, HEAD)
    scores = jnp.einsum(
        "agch,bgh->gcab", query_heads, keys_split, preferred_element_type=jnp.float32
    ) * (1.0 / math.sqrt(HEAD))
    allowed = key_ranks[None, :] <= query_ranks[:, None]
    masked = jnp.where(allowed, scores, -1e30)
    new_top = jnp.maximum(prev_top, jnp.max(masked, axis=-1))
    weights = jnp.where(allowed, jnp.exp(masked - new_top[..., None]), 0.0)
    factor = jnp.exp(prev_top - new_top)
    new_total = prev_total * factor + jnp.sum(weights, axis=-1)
    new_acc = prev_acc * factor[..., None] + jnp.einsum(
        "gcab,bgh->gcah",
        weights.astype(jnp.bfloat16),
        values_split,
        preferred_element_type=jnp.float32,
    )
    return (new_top, new_total, new_acc)


def make_fold(query_heads, query_ranks, rank_of, state, pieces):
    key_piece, value_piece = pieces
    length = key_piece.shape[0]

    def inner(block_turn, inner_state):
        block_start = block_turn * 512
        key_block = lax.dynamic_slice_in_dim(key_piece, block_start, 512, 0)
        value_block = lax.dynamic_slice_in_dim(value_piece, block_start, 512, 0)
        key_ranks = rank_of(block_start + jnp.arange(512, dtype=jnp.int32))
        return attend(query_heads, query_ranks, key_block, value_block, key_ranks, inner_state)

    return lax.fori_loop(0, length // 512, inner, state)


def body(
    hidden,
    kept_idx,
    kept_count,
    router,
    norm_gain,
    qk_gain,
    query_weight,
    key_weight,
    value_weight,
    out_weight,
):
    shard_count = lax.axis_size("blk")
    device = lax.axis_index("blk")
    width = hidden.shape[1]
    all_lists, all_counts = (
        lax.all_gather(kept_idx, "blk", axis=0, tiled=True),
        lax.all_gather(kept_count, "blk", axis=0, tiled=True),
    )
    starts = jnp.cumsum(all_counts) - all_counts
    own_start = starts[device]
    own_count = all_counts[device]
    list_slots = jnp.arange(CAP, dtype=jnp.int32)
    is_valid = list_slots < own_count
    token_rows = hidden[kept_idx[0]]
    gate_value = jax.nn.sigmoid(jnp.dot(token_rows, router, preferred_element_type=jnp.float32))
    slot_count = (CAP + shard_count - 1) // shard_count
    outgoing = jnp.where(is_valid[:, None], token_rows, jnp.zeros_like(token_rows))
    outgoing = jnp.roll(outgoing.reshape(slot_count, shard_count, width), own_start, axis=1)
    incoming = lax.all_to_all(outgoing, "blk", split_axis=1, concat_axis=1, tiled=True)
    query_ranks = device + jnp.arange(KEEP_DEV, dtype=jnp.int32) * shard_count
    source_ends = starts + all_counts
    source = jnp.sum((source_ends[None, :] <= query_ranks[:, None]).astype(jnp.int32), axis=1)
    within = query_ranks - starts[source]
    flat_index = within // shard_count * shard_count + source
    kept_rows = incoming.reshape(slot_count * shard_count, width)[flat_index]
    positions = source * TOK_DEV + all_lists[source, within]
    row_total = kept_rows.shape[0]
    normed = rms_scale(kept_rows.astype(jnp.float32), norm_gain).astype(jnp.bfloat16)
    query_cols = Q_HEADS * HEAD
    kv_cols = KV_HEADS * HEAD
    full_query, full_key, full_value, full_out = (
        lax.all_gather(query_weight, "blk", axis=0, tiled=True),
        lax.all_gather(key_weight, "blk", axis=0, tiled=True),
        lax.all_gather(value_weight, "blk", axis=0, tiled=True),
        lax.all_gather(out_weight, "blk", axis=0, tiled=True),
    )
    query_lin = jnp.dot(normed, full_query, preferred_element_type=jnp.float32)
    key_lin = jnp.dot(normed, full_key, preferred_element_type=jnp.float32)
    value_lin = jnp.dot(normed, full_value, preferred_element_type=jnp.float32)
    half_size = HEAD // 2
    rotation_rates = rope_base ** (-(jnp.arange(half_size, dtype=jnp.float32) * 2.0 / HEAD))
    angles = (positions.astype(jnp.float32)[:, None] * rotation_rates[None, :])[:, None, :]
    query_heads = rotate(
        rms_scale(query_lin.reshape(row_total, Q_HEADS, HEAD), qk_gain[0]), angles
    ).astype(jnp.bfloat16)
    key_heads = rotate(
        rms_scale(key_lin.reshape(row_total, KV_HEADS, HEAD), qk_gain[1]), angles
    ).astype(jnp.bfloat16)
    query_heads = query_heads.reshape(row_total, KV_HEADS, Q_HEADS // KV_HEADS, HEAD)
    key_flat = key_heads.reshape(row_total, kv_cols)
    value_flat = value_lin.astype(jnp.bfloat16)
    group_size = Q_HEADS // KV_HEADS
    start_state = (
        jnp.full((KV_HEADS, group_size, row_total), -1e30, jnp.float32),
        jnp.zeros((KV_HEADS, group_size, row_total), jnp.float32),
        jnp.zeros((KV_HEADS, group_size, row_total, HEAD), jnp.float32),
    )

    def strided_rank(slots_seen):
        return slots_seen // KEEP_DEV + slots_seen % KEEP_DEV * shard_count

    final_top, final_total, final_acc = make_fold(
        query_heads,
        query_ranks,
        strided_rank,
        start_state,
        (
            lax.all_gather(key_flat, "blk", axis=0, tiled=True),
            lax.all_gather(value_flat, "blk", axis=0, tiled=True),
        ),
    )
    attended = (
        (final_acc / final_total[..., None])
        .transpose(2, 0, 1, 3)
        .reshape(row_total, query_cols)
        .astype(jnp.bfloat16)
    )
    update = jnp.dot(attended, full_out, preferred_element_type=jnp.float32)
    update = update.astype(jnp.bfloat16)
    slot_grid = (
        jnp.arange(slot_count, dtype=jnp.int32)[:, None] * shard_count
        + jnp.mod(device - starts, shard_count)[None, :]
    )
    back_valid = slot_grid < all_counts[None, :]
    local_place = (starts[None, :] + slot_grid - device) // shard_count
    clipped = jnp.where(back_valid, local_place, 0)
    back_rows = jnp.where(back_valid[..., None], update[clipped], jnp.zeros((), jnp.bfloat16))
    returned = lax.all_to_all(back_rows, "blk", split_axis=1, concat_axis=1, tiled=True)
    returned = jnp.roll(returned, -own_start, axis=1).reshape(slot_count * shard_count, width)
    final = (
        token_rows.astype(jnp.float32) + gate_value[:, None] * returned.astype(jnp.float32)
    ).astype(jnp.bfloat16)
    target = jnp.where(is_valid, kept_idx[0], TOK_DEV)
    return hidden.at[target].set(final, mode="drop")


def solution(mesh):
    placed = (
        P(("groups", "blk"), None),
        P(("groups", "blk"), None),
        P(("groups", "blk")),
        P(),
        P(),
        P(),
        P("blk", None),
        P("blk", None),
        P("blk", None),
        P("blk", None),
    )
    return jax.shard_map(
        body, mesh=mesh, in_specs=placed, out_specs=P(("groups", "blk"), None), check_vma=False
    )
```

profile of v0, /device:TPU:0, one launch (start us, length us, event | category | flops | bytes accessed | tf_op | source)
XLA Modules:
  0.0 215.0 jit_solution(3244303445806012775)
XLA Ops:
  6.5 1.6 copy.93
  8.2 0.7 all-gather.6.cloned.1.call-update
  9.6 0.6 dynamic-slice
  10.2 0.7 dynamic-update-slice
  10.9 13.8 %all-reduce = s32[16]{0:T(128)S(1)} all-reduce(s32[16]{0:T(128)S(1)} %dynamic-update-slice), channel_id=1, replica_groups=mesh['groups'=2,'blk'=16] {'blk'}, use_global_device_ids=true, to_apply=%add | all-reduce | flops 16 | bytes 128
  25.0 0.6 dynamic_slice.30
  27.6 0.6 dynamic_slice.29
  28.9 0.9 gather_fusion
  30.8 1.0 fusion.30
  31.8 3.6 %all-to-all-start = ((bf16[8,16,2048]{2,0,1:T(8,128)(2,1)}), bf16[8,16,2048]{2,0,1:T(8,128)(2,1)S(1)}, u32[]{:S(2)}, u32[]{:S(2)}) async-start(bf16[8,16,2048]{2,0,1:T(8,128)(2,1)} %fusion.30), calls=%async_computation | async-start | bytes 1048576 | tf_op jit(solution)/shard_map/all_to_all | solution.py:102
  35.5 0.8 gather_fusion.1
  36.4 25.9 %all-gather = s32[16,1,128]{2,1,0:T(1,128)S(1)} all-gather(s32[1,1,128]{2,1,0:T(1,128)S(1)} %bitcast.125), channel_id=1, replica_groups=mesh['groups'=2,'blk'=16] {'blk'}, dimensions={0}, use_global_device_ids=true | all-gather | bytes 8704 | tf_op jit(solution)/shard_map/all_gather | solution.py:89
  62.3 0.8 gather_fusion.3
  63.5 23.3 %all_gather.29 = bf16[2048,128]{1,0:T(8,128)(2,1)S(1)} all-gather(bf16[128,128]{1,0:T(8,128)(2,1)S(1)} %copy-done.3), channel_id=1, replica_groups=mesh['groups'=2,'blk'=16] {'blk'}, dimensions={0}, use_global_device_ids=true | all-gather | bytes 557056 | tf_op jit(solution)/shard_map/all_gather | solution.py:117
  86.8 19.3 %all_gather.25 = bf16[2048,128]{1,0:T(8,128)(2,1)S(1)} all-gather(bf16[128,128]{1,0:T(8,128)(2,1)S(1)} %copy-done.4), channel_id=1, replica_groups=mesh['groups'=2,'blk'=16] {'blk'}, dimensions={0}, use_global_device_ids=true | all-gather | bytes 557056 | tf_op jit(solution)/shard_map/all_gather | solution.py:116
  106.4 0.7 gather_fusion.2
  108.7 20.5 %all_gather.30 = bf16[1024,128]{1,0:T(8,128)(2,1)S(1)} all-gather(bf16[64,128]{1,0:T(8,128)(2,1)S(1)} %convolution_convert_fusion.1), channel_id=1, replica_groups=mesh['groups'=2,'blk'=16] {'blk'}, dimensions={0}, use_global_device_ids=true | all-gather | bytes 278528 | tf_op jit(solution)/shard_map/all_gather | solution.py:152
  129.1 20.5 %all_gather.27 = bf16[1024,128]{1,0:T(8,128)(2,1)S(1)} all-gather(bf16[64,128]{1,0:T(8,128)(2,1)S(1)} %convert_element_type.65), channel_id=1, replica_groups=mesh['groups'=2,'blk'=16] {'blk'}, dimensions={0}, use_global_device_ids=true | all-gather | bytes 278528 | tf_op jit(solution)/shard_map/all_gather | solution.py:151
  149.6 5.0 %fusion.51 = f32[64,2048]{1,0:T(8,128)S(1)} fusion(bf16[2048,2048]{1,0:T(8,128)(2,1)} %all-gather.4.cloned.1.call-done, bf16[64,2048]{1,0:T(8,128)(2,1)S(1)} %gather_fusion.2, f32[2048]{0:T(1024)S(1)} %copy-done.2, f32[64]{0:T(128)S(1)} %add_rsqrt_fusion.2), kind=kOutput, calls=%fused_computation.132 | convolution fusion | flops 537395200 | bytes 9183488 | tf_op jit(solution)/shard_map/dot_general | solution.py:120
  157.1 19.5 %while.20 = (s32[]{:T(128)}, f32[2,16,64]{2,1,0:T(8,128)S(1)}, f32[2,16,64]{2,1,0:T(8,128)S(1)}, f32[2,16,64,64]{3,2,1,0:T(8,128)S(1)}, bf16[1024,128]{1,0:T(8,1...) while((s32[]{:T(128)}, f32[2,16,64]{2,1,0:T(8,128)S(1)}, ...), condition=%wide.region_8.10_spmd.clone, body=%wide.region_5.9_spmd.clone.sunk | while | flops 282514560 | bytes 15471291 | solution.py:70
  157.3 2.7 %fusion.79 = (f32[2,16,64]{2,1,0:T(8,128)S(1)}, f32[2,512,64,16]{1,2,3,0:T(8,128)}) fusion(pred[64,512]{1,0:T(8,128)(4,1)S(1)} %broadcast_compare_fusion.2, bf16[512,2,64,1]{0,2,3,1:T(8,128)(2,1)S(1)} %bitcast.117, bf16[64,2,16,64]{3,0,2,1:T(8,128)(2,1)S(1)} %get-tuple-element.414), kind=kOutput, calls=%fused_computation.9.clone.1 | convolution fusion | flops 137361408 | bytes 4628480 | tf_op jit(solution)/shard_map/while/body/eval_jaxpr/agch,bgh->gcab/dot_general | solution.py:41
  160.0 3.4 %fusion.80 = f32[2,16,64]{2,1,0:T(8,128)S(1)} fusion(f32[2,512,64,16]{1,2,3,0:T(8,128)} %get-tuple-element.381, f32[2,16,64]{2,1,0:T(8,128)S(1)} %select_maximum_fusion.2, pred[64,512]{1,0:T(8,128)(4,1)S(1)} %broadcast_compare_fusion.2), kind=kLoop, calls=%fused_computation.11.clone.1 | loop fusion | flops 5240832 | bytes 4243456 | tf_op jit(solution)/shard_map/while/body/eval_jaxpr/reduce_sum | solution.py:49
  163.6 3.1 %fusion.82 = f32[2,16,64,64]{3,2,1,0:T(8,128)S(1)} fusion(bf16[512,2,64,1]{0,2,3,1:T(8,128)(2,1)S(1)} %bitcast.120, f32[2,512,64,16]{1,2,3,0:T(8,128)} %get-tuple-element.381, f32[2,16,64]{2,1,0:T(8,128)S(1)} %select_maximum_fusion.2, pred[64,512]{1,0:T(8,128)(4,1)S(1)} %broadcast_compare_fusion.2, f32[2,16,64,64]{3,2,1,0:T(8,128)S(1)} %get-tuple-element.400, ...), kind=kOutput, calls=%fused_computation.14.clone.1 | convolution fusion | flops 139853824 | bytes 5423105 | tf_op jit(solution)/shard_map/while/body/eval_jaxpr/gcab,bgh->gcah/dot_general | solution.py:50
  167.0 2.7 %fusion.79 = (f32[2,16,64]{2,1,0:T(8,128)S(1)}, f32[2,512,64,16]{1,2,3,0:T(8,128)}) fusion(pred[64,512]{1,0:T(8,128)(4,1)S(1)} %broadcast_compare_fusion.2, bf16[512,2,64,1]{0,2,3,1:T(8,128)(2,1)S(1)} %bitcast.117, bf16[64,2,16,64]{3,0,2,1:T(8,128)(2,1)S(1)} %get-tuple-element.414), kind=kOutput, calls=%fused_computation.9.clone.1 | convolution fusion | flops 137361408 | bytes 4628480 | tf_op jit(solution)/shard_map/while/body/eval_jaxpr/agch,bgh->gcab/dot_general | solution.py:41
  169.7 3.5 %fusion.80 = f32[2,16,64]{2,1,0:T(8,128)S(1)} fusion(f32[2,512,64,16]{1,2,3,0:T(8,128)} %get-tuple-element.381, f32[2,16,64]{2,1,0:T(8,128)S(1)} %select_maximum_fusion.2, pred[64,512]{1,0:T(8,128)(4,1)S(1)} %broadcast_compare_fusion.2), kind=kLoop, calls=%fused_computation.11.clone.1 | loop fusion | flops 5240832 | bytes 4243456 | tf_op jit(solution)/shard_map/while/body/eval_jaxpr/reduce_sum | solution.py:49
  173.4 3.1 %fusion.82 = f32[2,16,64,64]{3,2,1,0:T(8,128)S(1)} fusion(bf16[512,2,64,1]{0,2,3,1:T(8,128)(2,1)S(1)} %bitcast.120, f32[2,512,64,16]{1,2,3,0:T(8,128)} %get-tuple-element.381, f32[2,16,64]{2,1,0:T(8,128)S(1)} %select_maximum_fusion.2, pred[64,512]{1,0:T(8,128)(4,1)S(1)} %broadcast_compare_fusion.2, f32[2,16,64,64]{3,2,1,0:T(8,128)S(1)} %get-tuple-element.400, ...), kind=kOutput, calls=%fused_computation.14.clone.1 | convolution fusion | flops 139853824 | bytes 5423105 | tf_op jit(solution)/shard_map/while/body/eval_jaxpr/gcab,bgh->gcah/dot_general | solution.py:50
  177.7 5.0 %convolution_convert_fusion = bf16[64,2048]{1,0:T(8,128)(2,1)S(1)} fusion(bf16[64,2048]{1,0:T(8,128)(2,1)S(1)} %convert_element_type.69, bf16[2048,2048]{1,0:T(8,128)(2,1)} %all-gather.6.cloned.1.call-done), kind=kOutput, calls=%fused_computation.38 | convolution fusion | flops 537001984 | bytes 8912896 | tf_op jit(solution)/shard_map/dot_general | solution.py:161
  182.7 0.9 gather_fusion.4
  183.6 1.1 copy_select_fusion
  184.7 3.8 %all-to-all-start.1 = ((bf16[8,16,2048]{2,0,1:T(8,128)(2,1)}), bf16[8,16,2048]{2,0,1:T(8,128)(2,1)S(1)}, u32[]{:S(2)}, u32[]{:S(2)}) async-start(bf16[8,16,2048]{2,0,1:T(8,128)(2,1)} %copy_select_fusion), calls=%async_computation.1 | async-start | bytes 1048576 | tf_op jit(solution)/shard_map/all_to_all | solution.py:171
  189.4 13.1 %all-to-all-done.1 = bf16[8,16,2048]{2,0,1:T(8,128)(2,1)S(1)} async-done(((bf16[8,16,2048]{2,0,1:T(8,128)(2,1)}), bf16[8,16,2048]{2,0,1:T(8,128)(2,1)S(1)}, u32[]{:S(2)}, u32[]{:S(2)}) %all-to-all-start.1) | async-done | bytes 524320 | tf_op jit(solution)/shard_map/all_to_all | solution.py:171
  203.6 4.6 %scatter_fusion = bf16[512,2048]{1,0:T(8,128)(2,1)} fusion(bf16[512,2048]{1,0:T(8,128)(2,1)} %copy-done, s32[128]{0:T(128)S(1)} %get-tuple-element.323, bf16[128,2048]{1,0:T(8,128)(2,1)S(1)} %fusion.24), kind=kCustom, calls=%fused_computation.5 | custom fusion | bytes 1573376 | tf_op jit(solution)/shard_map/scatter | solution.py:177
  (97 shorter events, 9.9 us)
Async XLA Ops:
  6.5 3.1 %copy-start.8 = (u32[32]{0:T(128)S(1)}, u32[32]{0:T(128)}, u32[]{:S(2)}) copy-start(u32[32]{0:T(128)} %constant.259) | copy-start | bytes 388
  6.5 21.7 %copy-start.6 = (s32[1,128]{1,0:T(1,128)S(1)}, s32[1,128]{1,0:T(1,128)}, u32[]{:S(2)}) copy-start(s32[1,128]{1,0:T(1,128)} %param.15) | copy-start | bytes 1540
  6.5 143.1 %all-gather.4.cloned.1.call-start = ((), (), s32[]{:S(2)}) async-start(), calls=%async_computation.2 | async-start | bytes 8912896 | tf_op jit(solution)/shard_map/all_gather | solution.py:115
  8.2 23.6 %copy-start = (bf16[512,2048]{1,0:T(8,128)(2,1)}, bf16[512,2048]{1,0:T(8,128)(2,1)S(1)}, u32[]{:S(2)}) copy-start(bf16[512,2048]{1,0:T(8,128)(2,1)S(1)} %copy.93) | copy-start | bytes 6291460
  8.2 169.5 %all-gather.6.cloned.1.call-start = ((), (), s32[]{:S(2)}) async-start(), calls=%async_computation.3 | async-start | bytes 8912896 | tf_op jit(solution)/shard_map/all_gather | solution.py:118
  28.8 34.3 %copy-start.7 = (f32[2,64]{1,0:T(2,128)S(1)}, f32[2,64]{1,0:T(2,128)}, u32[]{:S(2)}) copy-start(f32[2,64]{1,0:T(2,128)} %param.19) | copy-start | bytes 1540
  28.8 34.7 %copy-start.3 = (bf16[128,128]{1,0:T(8,128)(2,1)S(1)}, bf16[128,128]{1,0:T(8,128)(2,1)}, u32[]{:S(2)}) copy-start(bf16[128,128]{1,0:T(8,128)(2,1)} %param.22) | copy-start | bytes 98308
  28.9 57.9 %copy-start.4 = (bf16[128,128]{1,0:T(8,128)(2,1)S(1)}, bf16[128,128]{1,0:T(8,128)(2,1)}, u32[]{:S(2)}) copy-start(bf16[128,128]{1,0:T(8,128)(2,1)} %param.21) | copy-start | bytes 98308
  30.8 76.5 %copy-start.2 = (f32[2048]{0:T(1024)S(1)}, f32[2048]{0:T(1024)}, u32[]{:S(2)}) copy-start(f32[2048]{0:T(1024)} %param.18) | copy-start | bytes 24580
  31.8 74.3 %all-to-all-start = ((bf16[8,16,2048]{2,0,1:T(8,128)(2,1)}), bf16[8,16,2048]{2,0,1:T(8,128)(2,1)S(1)}, u32[]{:S(2)}, u32[]{:S(2)}) async-start(bf16[8,16,2048]{2,0,1:T(8,128)(2,1)} %fusion.30), calls=%async_computation | async-start | bytes 1048576 | tf_op jit(solution)/shard_map/all_to_all | solution.py:102
  155.4 1.6 copy-start.1
  182.7 6.5 %copy-start.5 = (bf16[2048]{0:T(1024)(128)(2,1)S(1)}, bf16[2048]{0:T(1024)(128)(2,1)}, u32[]{:S(2)}) copy-start(bf16[2048]{0:T(1024)(128)(2,1)} %param.17) | copy-start | bytes 12292
  184.7 17.8 %all-to-all-start.1 = ((bf16[8,16,2048]{2,0,1:T(8,128)(2,1)}), bf16[8,16,2048]{2,0,1:T(8,128)(2,1)S(1)}, u32[]{:S(2)}, u32[]{:S(2)}) async-start(bf16[8,16,2048]{2,0,1:T(8,128)(2,1)} %copy_select_fusion), calls=%async_computation.1 | async-start | bytes 1048576 | tf_op jit(solution)/shard_map/all_to_all | solution.py:171
Sparse Core Ops, SparseCore 0:
  9.5 84.1 all-gather.3
  95.8 77.4 all-gather.5
where the time goes:
time: 216 us; the launch traced here: 215 us
  blocking collectives  123 us (57%)
  matrix products  22.3 us (10%)
  between operations  17 us (8%)
  local copies, waits for them, and re-layouts  16.5 us (8%)
  other arithmetic  14.6 us (7%)
  waiting for transfers between devices  13.8 us (6%)
  starting transfers between devices  7.41 us (3%)
    all_gather x1, blocking collectives, body(): lax.all_gather(kept_idx, 'blk', axis=0, tiled=True)  25.9 us
    all_gather x1, blocking collectives, body(): lax.all_gather(value_weight, 'blk', axis=0, tiled=True)  23.3 us
    all_gather x1, blocking collectives, body(): lax.all_gather(value_flat, 'blk', axis=0, tiled=True)  20.5 us
    all_gather x1, blocking collectives, body(): lax.all_gather(key_flat, 'blk', axis=0, tiled=True)  20.5 us
    all_gather x1, blocking collectives, body(): lax.all_gather(key_weight, 'blk', axis=0, tiled=True)  19.3 us
    unnamed x1, blocking collectives  13.8 us
    all_to_all x1, waiting for transfers between devices, body(): lax.all_to_all(back_rows, 'blk', split_axis=1, concat_axis=1, tiled=True)  13.1 us
    reduce_sum x2, other arithmetic, attend(): new_total = prev_total * factor + jnp.sum(weights, axis=-1)  6.96 us
  transfers between devices with their start and end apart: 4, of which 1 were waited for; matrix products, arithmetic and copies ran while one was open for 18% of the time, Pallas kernels for 0%

commit v1 on v0

--- a/solution.py
+++ b/solution.py
@@ -168,7 +168,10 @@
     local_place = (starts[None, :] + slot_grid - device) // shard_count
     clipped = jnp.where(back_valid, local_place, 0)
     back_rows = jnp.where(back_valid[..., None], update[clipped], jnp.zeros((), jnp.bfloat16))
-    returned = lax.all_to_all(back_rows, "blk", split_axis=1, concat_axis=1, tiled=True)
+    returned = jnp.concatenate(
+        lax.all_to_all(jnp.stack(jnp.split(back_rows, lax.axis_size("blk"), axis=1)), "blk", 0, 0),
+        axis=1,
+    )
     returned = jnp.roll(returned, -own_start, axis=1).reshape(slot_count * shard_count, width)
     final = (
         token_rows.astype(jnp.float32) + gate_value[:, None] * returned.astype(jnp.float32)

time: 216 us -> 225 us (1.042)
  local copies, waits for them, and re-layouts: 16.5 us -> 26.2 us
    unnamed x23 -> x38, local copies, waits for them, and re-layouts: 3.01 us -> 12.1 us
  transfers between devices with their start and end apart: 4 -> 4, of which waited for: 1 -> 1; matrix products, arithmetic and copies ran while one was open for 18% -> 17% of each run, Pallas kernels for 0% -> 0%
where the time goes in v1:
time: 225 us; the launch traced here: 224 us
  blocking collectives  123 us (55%)
  local copies, waits for them, and re-layouts  26.2 us (12%)
  matrix products  22.3 us (10%)
  between operations  17 us (8%)
  waiting for transfers between devices  13.8 us (6%)
  other arithmetic  13.8 us (6%)
  starting transfers between devices  7.41 us (3%)
    all_gather x1, blocking collectives, body(): lax.all_gather(kept_idx, 'blk', axis=0, tiled=True)  25.9 us
    all_gather x1, blocking collectives, body(): lax.all_gather(value_weight, 'blk', axis=0, tiled=True)  23.3 us
    all_gather x1, blocking collectives, body(): lax.all_gather(value_flat, 'blk', axis=0, tiled=True)  20.5 us
    all_gather x1, blocking collectives, body(): lax.all_gather(key_flat, 'blk', axis=0, tiled=True)  20.5 us
    all_gather x1, blocking collectives, body(): lax.all_gather(key_weight, 'blk', axis=0, tiled=True)  19.3 us
    unnamed x1, blocking collectives  13.8 us
    all_to_all x1, waiting for transfers between devices, body(): lax.all_to_all(jnp.stack(jnp.split(back_rows, lax.axis_size('blk'), axis=...  13.1 us
    unnamed x38, local copies, waits for them, and re-layouts  12.1 us
  transfers between devices with their start and end apart: 4, of which 1 were waited for; matrix products, arithmetic and copies ran while one was open for 17% of the time, Pallas kernels for 0%

profile of v1, /device:TPU:0, one launch (start us, length us, event | category | flops | bytes accessed | tf_op | source)
XLA Modules:
  0.0 223.9 jit_solution(33316900938429207)
XLA Ops:
  6.5 1.6 copy.130
  8.2 0.7 all-gather.6.cloned.1.call-update
  9.6 0.6 dynamic-slice
  10.2 0.7 dynamic-update-slice
  10.9 13.8 %all-reduce = s32[16]{0:T(128)S(1)} all-reduce(s32[16]{0:T(128)S(1)} %dynamic-update-slice), channel_id=1, replica_groups=mesh['groups'=2,'blk'=16] {'blk'}, use_global_device_ids=true, to_apply=%add | all-reduce | flops 16 | bytes 128
  25.0 0.6 dynamic_slice.30
  27.6 0.6 dynamic_slice.29
  28.9 0.9 gather_fusion
  29.8 0.6 add_compare_fusion
  30.8 1.0 fusion.30
  31.8 3.6 %all-to-all-start = ((bf16[8,16,2048]{2,0,1:T(8,128)(2,1)}), bf16[8,16,2048]{2,0,1:T(8,128)(2,1)S(1)}, u32[]{:S(2)}, u32[]{:S(2)}) async-start(bf16[8,16,2048]{2,0,1:T(8,128)(2,1)} %fusion.30), calls=%async_computation | async-start | bytes 1048576 | tf_op jit(solution)/shard_map/all_to_all | solution.py:102
  35.5 0.8 gather_fusion.1
  36.4 25.9 %all-gather = s32[16,1,128]{2,1,0:T(1,128)S(1)} all-gather(s32[1,1,128]{2,1,0:T(1,128)S(1)} %bitcast.193), channel_id=1, replica_groups=mesh['groups'=2,'blk'=16] {'blk'}, dimensions={0}, use_global_device_ids=true | all-gather | bytes 8704 | tf_op jit(solution)/shard_map/all_gather | solution.py:89
  62.3 0.8 gather_fusion.3
  63.5 23.3 %all_gather.29 = bf16[2048,128]{1,0:T(8,128)(2,1)S(1)} all-gather(bf16[128,128]{1,0:T(8,128)(2,1)S(1)} %copy-done.3), channel_id=1, replica_groups=mesh['groups'=2,'blk'=16] {'blk'}, dimensions={0}, use_global_device_ids=true | all-gather | bytes 557056 | tf_op jit(solution)/shard_map/all_gather | solution.py:117
  86.8 19.3 %all_gather.25 = bf16[2048,128]{1,0:T(8,128)(2,1)S(1)} all-gather(bf16[128,128]{1,0:T(8,128)(2,1)S(1)} %copy-done.4), channel_id=1, replica_groups=mesh['groups'=2,'blk'=16] {'blk'}, dimensions={0}, use_global_device_ids=true | all-gather | bytes 557056 | tf_op jit(solution)/shard_map/all_gather | solution.py:116
  106.4 0.7 gather_fusion.2
  108.7 20.5 %all_gather.30 = bf16[1024,128]{1,0:T(8,128)(2,1)S(1)} all-gather(bf16[64,128]{1,0:T(8,128)(2,1)S(1)} %convolution_convert_fusion.1), channel_id=1, replica_groups=mesh['groups'=2,'blk'=16] {'blk'}, dimensions={0}, use_global_device_ids=true | all-gather | bytes 278528 | tf_op jit(solution)/shard_map/all_gather | solution.py:152
  129.1 20.5 %all_gather.27 = bf16[1024,128]{1,0:T(8,128)(2,1)S(1)} all-gather(bf16[64,128]{1,0:T(8,128)(2,1)S(1)} %convert_element_type.65), channel_id=1, replica_groups=mesh['groups'=2,'blk'=16] {'blk'}, dimensions={0}, use_global_device_ids=true | all-gather | bytes 278528 | tf_op jit(solution)/shard_map/all_gather | solution.py:151
  149.6 5.0 %fusion.67 = f32[64,2048]{1,0:T(8,128)S(1)} fusion(bf16[2048,2048]{1,0:T(8,128)(2,1)} %all-gather.4.cloned.1.call-done, bf16[64,2048]{1,0:T(8,128)(2,1)S(1)} %gather_fusion.2, f32[2048]{0:T(1024)S(1)} %copy-done.2, f32[64]{0:T(128)S(1)} %add_rsqrt_fusion.2), kind=kOutput, calls=%fused_computation.164 | convolution fusion | flops 537395200 | bytes 9183488 | tf_op jit(solution)/shard_map/dot_general | solution.py:120
  157.1 19.5 %while.20 = (s32[]{:T(128)}, f32[2,16,64]{2,1,0:T(8,128)S(1)}, f32[2,16,64]{2,1,0:T(8,128)S(1)}, f32[2,16,64,64]{3,2,1,0:T(8,128)S(1)}, bf16[1024,128]{1,0:T(8,1...) while((s32[]{:T(128)}, f32[2,16,64]{2,1,0:T(8,128)S(1)}, ...), condition=%wide.region_8.10_spmd.clone, body=%wide.region_5.9_spmd.clone.sunk | while | flops 282514560 | bytes 15471291 | solution.py:70
  157.3 2.7 %fusion.95 = (f32[2,16,64]{2,1,0:T(8,128)S(1)}, f32[2,512,64,16]{1,2,3,0:T(8,128)}) fusion(pred[64,512]{1,0:T(8,128)(4,1)S(1)} %broadcast_compare_fusion.2, bf16[512,2,64,1]{0,2,3,1:T(8,128)(2,1)S(1)} %bitcast.184, bf16[64,2,16,64]{3,0,2,1:T(8,128)(2,1)S(1)} %get-tuple-element.414), kind=kOutput, calls=%fused_computation.9.clone.1 | convolution fusion | flops 137361408 | bytes 4628480 | tf_op jit(solution)/shard_map/while/body/eval_jaxpr/agch,bgh->gcab/dot_general | solution.py:41
  160.0 3.4 %fusion.96 = f32[2,16,64]{2,1,0:T(8,128)S(1)} fusion(f32[2,512,64,16]{1,2,3,0:T(8,128)} %get-tuple-element.381, f32[2,16,64]{2,1,0:T(8,128)S(1)} %select_maximum_fusion.2, pred[64,512]{1,0:T(8,128)(4,1)S(1)} %broadcast_compare_fusion.2), kind=kLoop, calls=%fused_computation.11.clone.1 | loop fusion | flops 5240832 | bytes 4243456 | tf_op jit(solution)/shard_map/while/body/eval_jaxpr/reduce_sum | solution.py:49
  163.6 3.1 %fusion.98 = f32[2,16,64,64]{3,2,1,0:T(8,128)S(1)} fusion(bf16[512,2,64,1]{0,2,3,1:T(8,128)(2,1)S(1)} %bitcast.187, f32[2,512,64,16]{1,2,3,0:T(8,128)} %get-tuple-element.381, f32[2,16,64]{2,1,0:T(8,128)S(1)} %select_maximum_fusion.2, pred[64,512]{1,0:T(8,128)(4,1)S(1)} %broadcast_compare_fusion.2, f32[2,16,64,64]{3,2,1,0:T(8,128)S(1)} %get-tuple-element.400, ...), kind=kOutput, calls=%fused_computation.14.clone.1 | convolution fusion | flops 139853824 | bytes 5423105 | tf_op jit(solution)/shard_map/while/body/eval_jaxpr/gcab,bgh->gcah/dot_general | solution.py:50
  167.0 2.7 %fusion.95 = (f32[2,16,64]{2,1,0:T(8,128)S(1)}, f32[2,512,64,16]{1,2,3,0:T(8,128)}) fusion(pred[64,512]{1,0:T(8,128)(4,1)S(1)} %broadcast_compare_fusion.2, bf16[512,2,64,1]{0,2,3,1:T(8,128)(2,1)S(1)} %bitcast.184, bf16[64,2,16,64]{3,0,2,1:T(8,128)(2,1)S(1)} %get-tuple-element.414), kind=kOutput, calls=%fused_computation.9.clone.1 | convolution fusion | flops 137361408 | bytes 4628480 | tf_op jit(solution)/shard_map/while/body/eval_jaxpr/agch,bgh->gcab/dot_general | solution.py:41
  169.7 3.5 %fusion.96 = f32[2,16,64]{2,1,0:T(8,128)S(1)} fusion(f32[2,512,64,16]{1,2,3,0:T(8,128)} %get-tuple-element.381, f32[2,16,64]{2,1,0:T(8,128)S(1)} %select_maximum_fusion.2, pred[64,512]{1,0:T(8,128)(4,1)S(1)} %broadcast_compare_fusion.2), kind=kLoop, calls=%fused_computation.11.clone.1 | loop fusion | flops 5240832 | bytes 4243456 | tf_op jit(solution)/shard_map/while/body/eval_jaxpr/reduce_sum | solution.py:49
  173.4 3.1 %fusion.98 = f32[2,16,64,64]{3,2,1,0:T(8,128)S(1)} fusion(bf16[512,2,64,1]{0,2,3,1:T(8,128)(2,1)S(1)} %bitcast.187, f32[2,512,64,16]{1,2,3,0:T(8,128)} %get-tuple-element.381, f32[2,16,64]{2,1,0:T(8,128)S(1)} %select_maximum_fusion.2, pred[64,512]{1,0:T(8,128)(4,1)S(1)} %broadcast_compare_fusion.2, f32[2,16,64,64]{3,2,1,0:T(8,128)S(1)} %get-tuple-element.400, ...), kind=kOutput, calls=%fused_computation.14.clone.1 | convolution fusion | flops 139853824 | bytes 5423105 | tf_op jit(solution)/shard_map/while/body/eval_jaxpr/gcab,bgh->gcah/dot_general | solution.py:50
  177.7 5.0 %convolution_convert_fusion = bf16[64,2048]{1,0:T(8,128)(2,1)S(1)} fusion(bf16[64,2048]{1,0:T(8,128)(2,1)S(1)} %convert_element_type.69, bf16[2048,2048]{1,0:T(8,128)(2,1)} %all-gather.6.cloned.1.call-done), kind=kOutput, calls=%fused_computation.38 | convolution fusion | flops 537001984 | bytes 8912896 | tf_op jit(solution)/shard_map/dot_general | solution.py:161
  182.7 0.9 gather_fusion.4
  193.6 3.8 %all-to-all-start.1 = ((bf16[16,8,1,2048]{3,1,2,0:T(8,128)(2,1)}), bf16[16,8,1,2048]{3,1,2,0:T(8,128)(2,1)S(1)}, u32[]{:S(2)}, u32[]{:S(2)}) async-start(bf16[16,8,1,2048]{3,1,2,0:T(8,128)(2,1)} %fusion.32), calls=%async_computation.1 | async-start | bytes 1048576 | tf_op jit(solution)/shard_map/all_to_all | solution.py:172
  198.3 13.1 %all-to-all-done.1 = bf16[16,8,1,2048]{3,1,2,0:T(8,128)(2,1)S(1)} async-done(((bf16[16,8,1,2048]{3,1,2,0:T(8,128)(2,1)}), bf16[16,8,1,2048]{3,1,2,0:T(8,128)(2,1)S(1)}, u32[]{:S(2)}, u32[]{:S(2)}) %all-to-all-start.1) | async-done | bytes 524320 | tf_op jit(solution)/shard_map/all_to_all | solution.py:172
  212.5 4.6 %scatter_fusion = bf16[512,2048]{1,0:T(8,128)(2,1)} fusion(bf16[512,2048]{1,0:T(8,128)(2,1)} %copy-done, s32[128]{0:T(128)S(1)} %get-tuple-element.323, bf16[128,2048]{1,0:T(8,128)(2,1)S(1)} %fusion.24), kind=kCustom, calls=%fused_computation.5 | custom fusion | bytes 1573376 | tf_op jit(solution)/shard_map/scatter | solution.py:180
  (113 shorter events, 19.2 us)
Async XLA Ops:
  6.5 3.1 %copy-start.8 = (u32[32]{0:T(128)S(1)}, u32[32]{0:T(128)}, u32[]{:S(2)}) copy-start(u32[32]{0:T(128)} %constant.259) | copy-start | bytes 388
  6.5 21.7 %copy-start.6 = (s32[1,128]{1,0:T(1,128)S(1)}, s32[1,128]{1,0:T(1,128)}, u32[]{:S(2)}) copy-start(s32[1,128]{1,0:T(1,128)} %param.15) | copy-start | bytes 1540
  6.5 143.1 %all-gather.4.cloned.1.call-start = ((), (), s32[]{:S(2)}) async-start(), calls=%async_computation.2 | async-start | bytes 8912896 | tf_op jit(solution)/shard_map/all_gather | solution.py:115
  8.2 23.6 %copy-start = (bf16[512,2048]{1,0:T(8,128)(2,1)}, bf16[512,2048]{1,0:T(8,128)(2,1)S(1)}, u32[]{:S(2)}) copy-start(bf16[512,2048]{1,0:T(8,128)(2,1)S(1)} %copy.130) | copy-start | bytes 6291460
  8.2 169.5 %all-gather.6.cloned.1.call-start = ((), (), s32[]{:S(2)}) async-start(), calls=%async_computation.3 | async-start | bytes 8912896 | tf_op jit(solution)/shard_map/all_gather | solution.py:118
  28.8 34.3 %copy-start.7 = (f32[2,64]{1,0:T(2,128)S(1)}, f32[2,64]{1,0:T(2,128)}, u32[]{:S(2)}) copy-start(f32[2,64]{1,0:T(2,128)} %param.19) | copy-start | bytes 1540
  28.8 34.7 %copy-start.3 = (bf16[128,128]{1,0:T(8,128)(2,1)S(1)}, bf16[128,128]{1,0:T(8,128)(2,1)}, u32[]{:S(2)}) copy-start(bf16[128,128]{1,0:T(8,128)(2,1)} %param.22) | copy-start | bytes 98308
  28.9 57.9 %copy-start.4 = (bf16[128,128]{1,0:T(8,128)(2,1)S(1)}, bf16[128,128]{1,0:T(8,128)(2,1)}, u32[]{:S(2)}) copy-start(bf16[128,128]{1,0:T(8,128)(2,1)} %param.21) | copy-start | bytes 98308
  30.8 76.5 %copy-start.2 = (f32[2048]{0:T(1024)S(1)}, f32[2048]{0:T(1024)}, u32[]{:S(2)}) copy-start(f32[2048]{0:T(1024)} %param.18) | copy-start | bytes 24580
  31.8 74.3 %all-to-all-start = ((bf16[8,16,2048]{2,0,1:T(8,128)(2,1)}), bf16[8,16,2048]{2,0,1:T(8,128)(2,1)S(1)}, u32[]{:S(2)}, u32[]{:S(2)}) async-start(bf16[8,16,2048]{2,0,1:T(8,128)(2,1)} %fusion.30), calls=%async_computation | async-start | bytes 1048576 | tf_op jit(solution)/shard_map/all_to_all | solution.py:102
  155.4 1.6 copy-start.1
  182.7 15.4 %copy-start.5 = (bf16[2048]{0:T(1024)(128)(2,1)S(1)}, bf16[2048]{0:T(1024)(128)(2,1)}, u32[]{:S(2)}) copy-start(bf16[2048]{0:T(1024)(128)(2,1)} %param.17) | copy-start | bytes 12292
  193.6 17.8 %all-to-all-start.1 = ((bf16[16,8,1,2048]{3,1,2,0:T(8,128)(2,1)}), bf16[16,8,1,2048]{3,1,2,0:T(8,128)(2,1)S(1)}, u32[]{:S(2)}, u32[]{:S(2)}) async-start(bf16[16,8,1,2048]{3,1,2,0:T(8,128)(2,1)} %fusion.32), calls=%async_computation.1 | async-start | bytes 1048576 | tf_op jit(solution)/shard_map/all_to_all | solution.py:172
Sparse Core Ops, SparseCore 0:
  9.5 84.1 all-gather.3
  95.8 77.4 all-gather.5
